TPU v7x, 32 devices: a whole 2x2x4 slice. The times are simulated.
32 devices in a mesh: loop: 8 (over z, y), row: 4 (over x, core).
Axes of the slice: x: 2, y: 2, z: 4, core: 2. Of those that a mesh axis runs over, the one named last changes fastest.
Arguments:
- slab: float32 [2048, 16384], P('row', 'loop'), may hold values from -6 to 6
- rotations: float32 [32, 512, 512], P('loop', 'row')
- slab_pair: int32 [4], replicated, may hold values from 0 to 31, as said below
Outputs:
- moved: float32 [2048, 16384], P('row', 'loop')
Inputs may be any that keep to these rules, and one draw needn't show every extreme that they name: `slab_pair`: distinct pair numbers.
All inputs are finite; a program needn't handle non-finite values.
Results may differ from a plain program's by a relative error of at most 0.00009.
Values sent between devices are 32-bit elements; how exact they have to be, the bound alone decides.
No kernel may reach another device: no remote copies, remote signals or barrier semaphores. Data moves between devices by JAX's collectives and lax.ppermute only.
A program may use at most 64 MiB of HBM per device.

v0:
```python
import jax
import jax.numpy as jnp
from jax import lax
from jax.sharding import PartitionSpec as P


def from_behind(shard, axis, by):
    length = lax.axis_size(axis)
    pairs = [(i, i + by) for i in range(length) if 0 <= i + by < length]
    return lax.ppermute(shard, axis, pairs)


def from_root(shard, axis, root):
    mine = lax.axis_index(axis) == root
    return lax.psum(jnp.where(mine, shard, jnp.zeros_like(shard)), axis)


def left_apply(rotation, columns):
    return jnp.einsum("ij,in->jn", rotation, columns, precision=lax.Precision.HIGHEST)


def move_blocks(last_top, first_bottom):
    incoming_top = from_behind(last_top, "loop", 1)
    incoming_bottom = from_behind(first_bottom, "loop", -1)
    return (incoming_top, incoming_bottom)


def arrange(updated, incoming_top, incoming_bottom, pair_dev, half):
    rows = updated.shape[0]
    blocks = updated.reshape(rows, pair_dev, 2, half)
    tops = blocks[:, :, 0]
    bottoms = blocks[:, :, 1]
    new_tops = jnp.concatenate([incoming_top[:, None], tops[:, : pair_dev - 1]], axis=1)
    new_bottoms = jnp.concatenate([bottoms[:, 1:], incoming_bottom[:, None]], axis=1)
    place = lax.axis_index("loop") * pair_dev + jnp.arange(pair_dev, dtype=jnp.int32)
    total_pairs = pair_dev * lax.axis_size("loop")
    new_tops = jnp.where((place == 0)[None, :, None], tops, new_tops)
    new_tops = jnp.where((place == 1)[None, :, None], bottoms[:, :1], new_tops)
    new_bottoms = jnp.where(
        (place == total_pairs - 1)[None, :, None], tops[:, pair_dev - 1 :], new_bottoms
    )
    return jnp.stack([new_tops, new_bottoms], axis=2).reshape(rows, pair_dev * 2 * half)


def per_device(slab, rotations, slab_pair):
    pair_dev = rotations.shape[0]
    width = rotations.shape[2]
    half = width // 2
    rows = slab.shape[0]
    panels = slab.reshape(rows, pair_dev, width)
    wanted = slab_pair[lax.axis_index("row")]
    local_slot = wanted % pair_dev
    owner = wanted // pair_dev
    gathered = lax.all_gather(rotations, "row", axis=1, tiled=True)
    turned = jnp.einsum("rpi,pij->rpj", panels, gathered, precision=lax.Precision.HIGHEST)
    picked = lax.dynamic_index_in_dim(gathered, local_slot, 0, keepdims=False)
    rotation = from_root(picked, "loop", owner)
    flat = turned.reshape(rows, pair_dev * width)
    updated = left_apply(rotation, flat)
    last_top = updated[:, (pair_dev - 1) * width : (pair_dev - 1) * width + half]
    first_bottom = updated[:, half:width]
    incoming_top, incoming_bottom = move_blocks(last_top, first_bottom)
    return arrange(updated, incoming_top, incoming_bottom, pair_dev, half)


def solution(mesh):
    return jax.shard_map(
        per_device,
        mesh=mesh,
        in_specs=(P("row", "loop"), P("loop", "row", None), P()),
        out_specs=P("row", "loop"),
        check_vma=False,
    )
```

profile of v0, /device:TPU:0, one launch (start us, length us, event | category | flops | bytes accessed | tf_op | source)
XLA Modules:
  0.0 199.6 jit_solution(9748989037205450885)
XLA Ops:
  6.5 2.5 %copy.13 = f32[4,128,512]{1,2,0:T(8,128)} copy(f32[4,128,512]{2,1,0:T(8,128)} %param.4) | data formatting | bytes 2097152 | tf_op args[1]
  9.2 0.7 dynamic_slice.7
  12.6 34.4 %all-gather.2.cloned.1.call-done = f32[4,512,512]{1,2,0:T(8,128)} async-done(((f32[4,128,512]{1,2,0:T(8,128)}), f32[4,512,512]{1,2,0:T(8,128)}) %all-gather.2.cloned.1.call-update) | async-done | bytes 4194320 | tf_op jit(solution)/shard_map/all_gather | solution.py:54
  47.0 2.3 %select_bitcast_fusion = f32[512,512]{0,1:T(8,128)} fusion(f32[4,512,512]{1,2,0:T(8,128)} %all-gather.2.cloned.1.call-done, s32[]{:T(128)S(6)} %select_n.53, pred[]{:T(512)S(6)} %eq.27), kind=kLoop, calls=%fused_computation.11 | loop fusion | flops 262144 | bytes 2097157 | tf_op jit(solution)/shard_map/jit(_where)/select_n | solution.py:15
  49.4 12.0 %fusion = f32[4,512,512]{2,1,0:T(8,128)} fusion(f32[4,512,512]{1,2,0:T(8,128)} %all-gather.2.cloned.1.call-done, f32[64,4,8,512]{3,2,1,0:T(8,128)} %bitcast.36), kind=kOutput, calls=%fused_computation | convolution fusion | flops 6442450944 | bytes 12582912 | tf_op jit(solution)/shard_map/rpi,pij->rpj/dot_general | solution.py:55
  61.4 67.1 %all-reduce.2.cloned.1.call-done = f32[512,512]{0,1:T(8,128)} async-done(((f32[512,512]{0,1:T(8,128)}), f32[512,512]{0,1:T(8,128)}) %all-reduce.2.cloned.1.call-update) | async-done | bytes 1048592 | tf_op jit(solution)/shard_map/psum | solution.py:15
  128.5 9.0 %fusion.9 = f32[512,2048]{1,0:T(8,128)S(1)} fusion(f32[512,512]{0,1:T(8,128)} %all-reduce.2.cloned.1.call-done, f32[512,2048]{0,1:T(8,128)} %bitcast.30), kind=kOutput, calls=%fused_computation.20 | convolution fusion | flops 6442450944 | bytes 9437184 | tf_op jit(solution)/shard_map/ij,in->jn/dot_general | solution.py:19
  137.6 2.0 %copy-done = f32[512,2048]{1,0:T(8,128)} copy-done((f32[512,2048]{1,0:T(8,128)}, f32[512,2048]{1,0:T(8,128)S(1)}, u32[]{:S(2)}) %copy-start) | copy-done | bytes 4194328
  139.6 0.1 fusion.7
  139.7 6.6 %reshape.61 = f32[512,4,2,256]{3,2,1,0:T(2,128)} reshape(f32[512,2048]{1,0:T(8,128)} %copy-done) | data formatting | bytes 8388608 | tf_op jit(solution)/shard_map/reshape | solution.py:30
  146.3 7.1 %fusion.8 = (f32[512,4,1,256]{3,2,1,0:T(1,128)S(1)}, f32[512,4,1,256]{3,2,1,0:T(1,128)S(1)}) fusion(f32[512,4,2,256]{3,2,1,0:T(2,128)} %reshape.61), kind=kLoop, calls=%fused_computation.19 | loop fusion | bytes 8388608 | tf_op jit(solution)/shard_map/slice | solution.py:31
  153.3 0.4 copy.29
  153.8 0.1 slice_bitcast_fusion
  153.9 3.2 %collective-permute-start = (f32[512,256]{1,0:T(8,128)S(1)}, f32[512,256]{1,0:T(8,128)S(1)}, u32[]{:S(2)}, u32[]{:S(2)}) collective-permute-start(f32[512,256]{1,0:T(8,128)S(1)} %get-tuple-element.5), channel_id=1, source_target_pairs={{0,4},{4,8},{8,12},{12,16},{16,20},{20,24},{24,28},{1,5},{5,9},{9,... | collective-permute-start | bytes 1572872 | tf_op jit(solution)/shard_map/ppermute | solution.py:10
  157.1 1.3 collective-permute-start.1
  158.4 0.4 copy.30
  158.8 0.1 slice_bitcast_fusion.1
  159.0 13.0 %collective-permute-done.1 = f32[512,256]{1,0:T(8,128)S(1)} collective-permute-done((f32[512,256]{1,0:T(8,128)S(1)}, f32[512,256]{1,0:T(8,128)S(1)}, u32[]{:S(2)}, u32[]{:S(2)}) %collective-permute-start.1) | collective-permute-done | bytes 524320 | tf_op jit(solution)/shard_map/ppermute | solution.py:10
  172.0 0.2 maximum_select_fusion.1
  172.3 6.8 %collective-permute-done = f32[512,256]{1,0:T(8,128)S(1)} collective-permute-done((f32[512,256]{1,0:T(8,128)S(1)}, f32[512,256]{1,0:T(8,128)S(1)}, u32[]{:S(2)}, u32[]{:S(2)}) %collective-permute-start) | collective-permute-done | bytes 524320 | tf_op jit(solution)/shard_map/ppermute | solution.py:10
  179.1 0.6 fusion.3
  179.7 2.5 %pad_maximum_fusion = f32[512,4,2,256]{3,0,2,1:T(8,128)} fusion(f32[512,4,1,256]{3,0,2,1:T(8,128)S(1)} %maximum_select_fusion.1, f32[512,4,1,256]{3,0,2,1:T(8,128)S(1)} %fusion.3), kind=kLoop, calls=%fused_computation.3 | loop fusion | flops 1048576 | bytes 8388608 | tf_op jit(solution)/shard_map/stack | solution.py:42
  182.2 5.2 %copy.17 = f32[512,4,2,256]{0,3,2,1:T(8,128)} copy(f32[512,4,2,256]{3,0,2,1:T(8,128)} %pad_maximum_fusion) | data formatting | bytes 8388608 | tf_op jit(solution)/shard_map/stack | solution.py:42
  187.4 5.3 %copy.18 = f32[512,2048]{1,0:T(8,128)} copy(f32[512,2048]{0,1:T(8,128)} %bitcast.31) | data formatting | bytes 8388608 | tf_op jit(solution)/shard_map/reshape | solution.py:42
  (11 shorter events, 0.2 us)
Async XLA Ops:
  6.5 2.6 %copy-start.1 = (s32[4]{0:T(128)S(1)}, s32[4]{0:T(128)}, u32[]{:S(2)}) copy-start(s32[4]{0:T(128)} %param.5) | copy-start | bytes 52
  6.5 40.4 %all-gather.2.cloned.1.call-start = ((), (), s32[]{:S(2)}) async-start(), calls=%async_computation | async-start | bytes 5242880 | tf_op jit(solution)/shard_map/all_gather | solution.py:54
  9.1 119.4 %all-reduce.2.cloned.1.call-start = ((), (), s32[]{:S(2)}) async-start(), calls=%async_computation.1 | async-start | bytes 2097152 | tf_op jit(solution)/shard_map/psum | solution.py:15
  137.6 2.0 %copy-start = (f32[512,2048]{1,0:T(8,128)}, f32[512,2048]{1,0:T(8,128)S(1)}, u32[]{:S(2)}) copy-start(f32[512,2048]{1,0:T(8,128)S(1)} %fusion.9) | copy-start | bytes 12582916
  153.9 25.2 %collective-permute-start = (f32[512,256]{1,0:T(8,128)S(1)}, f32[512,256]{1,0:T(8,128)S(1)}, u32[]{:S(2)}, u32[]{:S(2)}) collective-permute-start(f32[512,256]{1,0:T(8,128)S(1)} %get-tuple-element.5), channel_id=1, source_target_pairs={{0,4},{4,8},{8,12},{12,16},{16,20},{20,24},{24,28},{1,5},{5,9},{9,... | collective-permute-start | bytes 1572872 | tf_op jit(solution)/shard_map/ppermute | solution.py:10
  157.1 14.9 %collective-permute-start.1 = (f32[512,256]{1,0:T(8,128)S(1)}, f32[512,256]{1,0:T(8,128)S(1)}, u32[]{:S(2)}, u32[]{:S(2)}) collective-permute-start(f32[512,256]{1,0:T(8,128)S(1)} %get-tuple-element.6), channel_id=1, source_target_pairs={{4,0},{8,4},{12,8},{16,12},{20,16},{24,20},{28,24},{5,1},{9,5},{13... | collective-permute-start | bytes 1572872 | tf_op jit(solution)/shard_map/ppermute | solution.py:10
Sparse Core Ops, SparseCore 0:
  9.2 37.7 all-gather.1
  50.5 77.9 all-reduce.1
where the time goes:
time: 200 us
  waiting for transfers between devices  121 us (60%)
  local copies, waits for them, and re-layouts  30.6 us (15%)
  matrix products  21.1 us (11%)
  between operations  16.3 us (8%)
  other arithmetic  5.63 us (3%)
  starting transfers between devices  4.53 us (2%)
    psum x1, waiting for transfers between devices, from_root(): return lax.psum(jnp.where(mine, shard, jnp.zeros_like(shard)), axis)  67.1 us
    all_gather x1, waiting for transfers between devices, per_device(): gathered = lax.all_gather(rotations, 'row', axis=1, tiled=True)  34.4 us
    ppermute x2, waiting for transfers between devices, from_behind(): return lax.ppermute(shard, axis, pairs)  19.9 us
    dot_general x1, matrix products, per_device(): jnp.einsum('rpi,pij->rpj', panels, gathered, precision=lax.Precision.HIGH...  12 us
    dot_general x1, matrix products, left_apply(): jnp.einsum('ij,in->jn', rotation, columns, precision=lax.Precision.HIGHEST)  9.04 us
    slice x1, local copies, waits for them, and re-layouts, arrange(): tops = blocks[:, :, 0]  7.06 us
    reshape x1, local copies, waits for them, and re-layouts, arrange(): blocks = updated.reshape(rows, pair_dev, 2, half)  6.59 us
    unnamed x7, local copies, waits for them, and re-layouts  5.36 us
  transfers between devices with their start and end apart: 4, of which 4 were waited for; matrix products, arithmetic and copies ran while one was open for 7% of the time, Pallas kernels for 0%

commit v1 on v0

--- a/solution.py
+++ b/solution.py
@@ -12,7 +12,7 @@
 
 def from_root(shard, axis, root):
     mine = lax.axis_index(axis) == root
-    return lax.psum(jnp.where(mine, shard, jnp.zeros_like(shard)), axis)
+    return jnp.sum(lax.all_gather(jnp.where(mine, shard, jnp.zeros_like(shard)), axis), axis=0)
 
 
 def left_apply(rotation, columns):

time: 200 us -> 250 us (1.25)
  waiting for transfers between devices: 121 us -> 159 us
  matrix products: 21.1 us -> 27.1 us
  other arithmetic: 5.63 us -> 9.11 us
    all_gather x0 -> x1, waiting for transfers between devices: none -> 113 us  [from_root(): lax.all_gather(jnp.where(mine, shard, jnp.zeros_like(shard)), axis)]
    psum x1 -> x0, waiting for transfers between devices: 67.1 us -> none  [from_root(): return lax.psum(jnp.where(mine, shard, jnp.zeros_like(shard)), axis)]
    ppermute x2, waiting for transfers between devices: 19.9 us -> 11 us  [from_behind(): return lax.ppermute(shard, axis, pairs)]
    dot_general x1, matrix products: 9.04 us -> 15.1 us  [left_apply(): jnp.einsum('ij,in->jn', rotation, columns, precision=lax.Precision.HIGHEST)]
    unnamed x0 -> x1, other arithmetic: none -> 4.49 us
  transfers between devices with their start and end apart: 4 -> 4, of which waited for: 4 -> 4; matrix products, arithmetic and copies ran while one was open for 7% -> 8% of each run, Pallas kernels for 0% -> 0%
where the time goes in v1:
time: 250 us; the launch traced here: 249 us
  waiting for transfers between devices  159 us (64%)
  local copies, waits for them, and re-layouts  32.1 us (13%)
  matrix products  27.1 us (11%)
  between operations  16.1 us (6%)
  other arithmetic  9.11 us (4%)
  starting transfers between devices  5.9 us (2%)
    all_gather x1, waiting for transfers between devices, from_root(): lax.all_gather(jnp.where(mine, shard, jnp.zeros_like(shard)), axis)  113 us
    all_gather x1, waiting for transfers between devices, per_device(): gathered = lax.all_gather(rotations, 'row', axis=1, tiled=True)  34.6 us
    dot_general x1, matrix products, left_apply(): jnp.einsum('ij,in->jn', rotation, columns, precision=lax.Precision.HIGHEST)  15.1 us
    dot_general x1, matrix products, per_device(): jnp.einsum('rpi,pij->rpj', panels, gathered, precision=lax.Precision.HIGH...  12 us
    ppermute x2, waiting for transfers between devices, from_behind(): return lax.ppermute(shard, axis, pairs)  11 us
    slice x1, local copies, waits for them, and re-layouts, arrange(): tops = blocks[:, :, 0]  7.06 us
    reshape x1, local copies, waits for them, and re-layouts, arrange(): blocks = updated.reshape(rows, pair_dev, 2, half)  6.77 us
    ppermute x2, starting transfers between devices, from_behind(): return lax.ppermute(shard, axis, pairs)  5.86 us
  transfers between devices with their start and end apart: 4, of which 4 were waited for; matrix products, arithmetic and copies ran while one was open for 8% of the time, Pallas kernels for 0%

profile of v1, /device:TPU:0, one launch (start us, length us, event | category | flops | bytes accessed | tf_op | source)
XLA Modules:
  0.0 249.1 jit_solution(6507099863333137205)
XLA Ops:
  6.5 2.5 %copy.19 = f32[4,128,512]{1,2,0:T(8,128)} copy(f32[4,128,512]{2,1,0:T(8,128)} %param.4) | data formatting | bytes 2097152 | tf_op args[1]
  9.2 0.6 dynamic_slice.7
  12.4 34.6 %all-gather.3.cloned.1.call-done = f32[4,512,512]{1,2,0:T(8,128)} async-done(((f32[4,128,512]{1,2,0:T(8,128)}), f32[4,512,512]{1,2,0:T(8,128)}) %all-gather.3.cloned.1.call-update) | async-done | bytes 4194320 | tf_op jit(solution)/shard_map/all_gather | solution.py:54
  47.0 1.3 dynamic-slice_select_fusion
  48.3 1.4 copy.20
  49.7 12.0 %fusion = f32[4,512,512]{2,1,0:T(8,128)} fusion(f32[4,512,512]{1,2,0:T(8,128)} %all-gather.3.cloned.1.call-done, f32[64,4,8,512]{3,2,1,0:T(8,128)} %bitcast.34), kind=kOutput, calls=%fused_computation | convolution fusion | flops 6442450944 | bytes 12582912 | tf_op jit(solution)/shard_map/rpi,pij->rpj/dot_general | solution.py:55
  61.8 113.0 %all-gather.5.cloned.1.call-done = f32[8,512,512]{2,1,0:T(8,128)} async-done(((f32[1,512,512]{2,1,0:T(8,128)}), f32[8,512,512]{2,1,0:T(8,128)}) %all-gather.5.cloned.1.call-update) | async-done | bytes 8388624 | tf_op jit(solution)/shard_map/all_gather | solution.py:15
  174.8 4.5 %reduce_sum.9 = f32[512,512]{1,0:T(8,128)S(1)} reduce(f32[8,512,512]{2,1,0:T(8,128)} %all-gather.5.cloned.1.call-done, f32[]{:T(128)} %constant.45.clone.1), dimensions={0}, to_apply=%region_0.1 | reduce | flops 1835008 | bytes 9437188
  179.3 15.1 %fusion.9 = f32[512,2048]{1,0:T(8,128)S(1)} fusion(f32[512,512]{1,0:T(8,128)S(1)} %reduce_sum.9, f32[512,2048]{0,1:T(8,128)} %bitcast.28), kind=kOutput, calls=%fused_computation.20 | convolution fusion | flops 6442450944 | bytes 9437184 | tf_op jit(solution)/shard_map/ij,in->jn/dot_general | solution.py:19
  194.4 2.0 copy-done
  196.5 6.8 %reshape.58 = f32[512,4,2,256]{3,2,1,0:T(2,128)} reshape(f32[512,2048]{1,0:T(8,128)} %copy-done) | data formatting | bytes 8388608 | tf_op jit(solution)/shard_map/reshape | solution.py:30
  203.3 1.3 collective-permute-start.1
  204.6 7.1 %fusion.8 = (f32[512,4,1,256]{3,2,1,0:T(1,128)S(1)}, f32[512,4,1,256]{3,2,1,0:T(1,128)S(1)}) fusion(f32[512,4,2,256]{3,2,1,0:T(2,128)} %reshape.58), kind=kLoop, calls=%fused_computation.19 | loop fusion | bytes 8388608 | tf_op jit(solution)/shard_map/slice | solution.py:31
  211.6 0.4 copy.38
  212.1 0.1 slice_bitcast_fusion
  212.2 0.4 copy.39
  212.7 4.6 %collective-permute-start = (f32[512,256]{1,0:T(8,128)S(1)}, f32[512,256]{1,0:T(8,128)S(1)}, u32[]{:S(2)}, u32[]{:S(2)}) collective-permute-start(f32[512,256]{1,0:T(8,128)S(1)} %get-tuple-element.5), channel_id=1, source_target_pairs={{0,4},{4,8},{8,12},{12,16},{16,20},{20,24},{24,28},{1,5},{5,9},{9,... | collective-permute-start | bytes 1572872 | tf_op jit(solution)/shard_map/ppermute | solution.py:10
  217.4 1.1 collective-permute-done.1
  218.4 0.2 maximum_select_fusion.1
  218.7 10.0 %collective-permute-done = f32[512,256]{1,0:T(8,128)S(1)} collective-permute-done((f32[512,256]{1,0:T(8,128)S(1)}, f32[512,256]{1,0:T(8,128)S(1)}, u32[]{:S(2)}, u32[]{:S(2)}) %collective-permute-start) | collective-permute-done | bytes 524320 | tf_op jit(solution)/shard_map/ppermute | solution.py:10
  228.6 0.6 fusion.3
  229.2 2.5 pad_maximum_fusion
  231.7 5.2 %copy.25 = f32[512,4,2,256]{0,3,2,1:T(8,128)} copy(f32[512,4,2,256]{3,0,2,1:T(8,128)} %pad_maximum_fusion) | data formatting | bytes 8388608 | tf_op jit(solution)/shard_map/stack | solution.py:42
  236.9 5.3 %copy.26 = f32[512,2048]{1,0:T(8,128)} copy(f32[512,2048]{0,1:T(8,128)} %bitcast.29) | data formatting | bytes 8388608 | tf_op jit(solution)/shard_map/reshape | solution.py:42
  (13 shorter events, 0.4 us)
Async XLA Ops:
  6.5 2.6 %copy-start.1 = (s32[4]{0:T(128)S(1)}, s32[4]{0:T(128)}, u32[]{:S(2)}) copy-start(s32[4]{0:T(128)} %param.5) | copy-start | bytes 52
  6.5 40.4 %all-gather.3.cloned.1.call-start = ((), (), s32[]{:S(2)}) async-start(), calls=%async_computation | async-start | bytes 5242880 | tf_op jit(solution)/shard_map/all_gather | solution.py:54
  9.1 165.7 %all-gather.5.cloned.1.call-start = ((), (), s32[]{:S(2)}) async-start(), calls=%async_computation.1 | async-start | bytes 9437184 | tf_op jit(solution)/shard_map/all_gather | solution.py:15
  194.4 2.0 copy-start
  203.3 15.1 %collective-permute-start.1 = (f32[512,256]{1,0:T(8,128)S(1)}, f32[512,256]{1,0:T(8,128)S(1)}, u32[]{:S(2)}, u32[]{:S(2)}) collective-permute-start(f32[512,256]{1,0:T(8,128)S(1)} %get-tuple-element.6), channel_id=1, source_target_pairs={{4,0},{8,4},{12,8},{16,12},{20,16},{24,20},{28,24},{5,1},{9,5},{13... | collective-permute-start | bytes 1572872 | tf_op jit(solution)/shard_map/ppermute | solution.py:10
  212.7 15.9 %collective-permute-start = (f32[512,256]{1,0:T(8,128)S(1)}, f32[512,256]{1,0:T(8,128)S(1)}, u32[]{:S(2)}, u32[]{:S(2)}) collective-permute-start(f32[512,256]{1,0:T(8,128)S(1)} %get-tuple-element.5), channel_id=1, source_target_pairs={{0,4},{4,8},{8,12},{12,16},{16,20},{20,24},{24,28},{1,5},{5,9},{9,... | collective-permute-start | bytes 1572872 | tf_op jit(solution)/shard_map/ppermute | solution.py:10
Sparse Core Ops, SparseCore 0:
  9.2 37.7 all-gather.2
  49.8 124.9 all-gather.4
